TPU v7x, 32 devices: a whole 2x2x4 slice. The times are simulated.
32 devices in a mesh: dp: 8 (over z, y), mp: 4 (over x, core).
Axes of the slice: x: 2, y: 2, z: 4, core: 2. Of those that a mesh axis runs over, the one named last changes fastest.
Arguments:
- latents: bfloat16 [262144, 256], P(('dp', 'mp')), may hold values from -6 to 6
- proj_weight: bfloat16 [18, 256], replicated, may hold values from -0.375 to 0.375
- proj_bias: float32 [18], replicated, may hold values from -2.5 to 2.5
- fill: int32 [2048], replicated, may hold values from 0 to 128, as said below
- target: int32 [2048], replicated, may hold values from -1 to 7, as said below
- target_slot: int32 [2048], replicated, may hold values from -1 to 31, as said below
Outputs:
- latent_grad: bfloat16 [131072, 256], P(('dp', 'mp'))
- weight_grad: float32 [18, 256], replicated
- entropy_loss: float32 [], replicated
Inputs may be any that keep to these rules, and one draw needn't show every extreme that they name: `fill`: zero exactly on the empty slots of a device, which are those whose target is -1. `target`: blocks go to devices with the same mp index. Each device receives exactly 32 blocks, one in each of its positions; at most 8 blocks goes from one device to any one index of dp, and some device does send 8 block to an index. -1 marks an empty slot. `target_slot`: -1 exactly where target is -1.
All inputs are finite; a program needn't handle non-finite values.
Results may differ from a plain program's by a relative error of at most 0.0049.
Values may be sent and summed in bfloat16 or wider, within the bound.
A program may use at most 64 MiB of HBM per device.

v0:
```python
import jax
import jax.numpy as jnp
from jax import lax
from jax.sharding import PartitionSpec as P

BLK = 128
OUT_SLOTS = 32
sharpness = 2.0


def routing(fill, target, target_slot, n_dp, n_mp, in_slots, capacity, own_dp, own_mp):
    col_shape = (n_dp, n_mp, in_slots)
    col_fill = lax.dynamic_index_in_dim(fill.reshape(col_shape), own_mp, 1, keepdims=False)
    col_target = lax.dynamic_index_in_dim(target.reshape(col_shape), own_mp, 1, keepdims=False)
    col_slot = lax.dynamic_index_in_dim(target_slot.reshape(col_shape), own_mp, 1, keepdims=False)
    matches = col_target[:, :, None] == col_target[:, None, :]
    earlier = lax.broadcasted_iota(jnp.int32, (in_slots, in_slots), 0) < lax.broadcasted_iota(
        jnp.int32, (in_slots, in_slots), 1
    )
    arrival_rank = jnp.sum((matches & earlier[None]).astype(jnp.int32), axis=1)
    sources = lax.broadcasted_iota(jnp.int32, (n_dp, in_slots), 0)
    arrive = sources * capacity + arrival_rank
    own_target = lax.dynamic_index_in_dim(col_target, own_dp, 0, keepdims=False)
    own_rank = lax.dynamic_index_in_dim(arrival_rank, own_dp, 0, keepdims=False)
    send_slot = jnp.where(own_target >= 0, own_target * capacity + own_rank, n_dp * capacity)
    chosen = (
        jnp.full((n_dp * capacity,), in_slots, jnp.int32)
        .at[send_slot]
        .set(jnp.arange(in_slots, dtype=jnp.int32), mode="drop")
    )
    landing = jnp.where(col_target == own_dp, col_slot, OUT_SLOTS).reshape(-1)
    gather_order = (
        jnp.zeros((OUT_SLOTS,), jnp.int32).at[landing].set(arrive.reshape(-1), mode="drop")
    )
    out_fill = jnp.zeros((OUT_SLOTS,), jnp.int32).at[landing].set(col_fill.reshape(-1), mode="drop")
    own_fill = lax.dynamic_index_in_dim(col_fill, own_dp, 0, keepdims=False)
    return (chosen, gather_order, out_fill, own_fill)


def statistics(blocks, fills, proj_weight, proj_bias):
    logits = (
        jnp.einsum("nkd,bd->nbk", blocks, proj_weight, preferred_element_type=jnp.float32)
        + proj_bias[None, :, None]
    )
    scaled = sharpness * logits
    token_mask = (lax.broadcasted_iota(jnp.int32, (1, 1, BLK), 2) < fills[:, None, None]).astype(
        jnp.float32
    )
    probability = jax.nn.sigmoid(scaled)
    entropy = jax.nn.softplus(scaled) - probability * scaled
    bit_sums = jnp.sum(probability * token_mask, axis=(0, 2))
    entropy_sum = jnp.sum(entropy * token_mask)
    variance = probability * (1.0 - probability) * token_mask
    return (bit_sums, entropy_sum, -2.0 * scaled * variance, 2.0 * variance)


def local(latents, proj_weight, proj_bias, fill, target, target_slot):
    n_dp = lax.axis_size("dp")
    n_mp = lax.axis_size("mp")
    own_dp = lax.axis_index("dp")
    own_mp = lax.axis_index("mp")
    feature_width = latents.shape[1]
    in_slots = latents.shape[0] // BLK
    capacity = max(1, 2 * OUT_SLOTS // n_dp)
    chosen, gather_order, out_fill, own_fill = routing(
        fill, target, target_slot, n_dp, n_mp, in_slots, capacity, own_dp, own_mp
    )
    token_count = jnp.sum(fill).astype(jnp.float32)
    loaded = latents.reshape(in_slots, BLK, feature_width)
    bit_sums, entropy_sum, first_term, second_term = statistics(
        loaded, own_fill, proj_weight, proj_bias
    )
    first_rounded = first_term.astype(jnp.bfloat16)
    second_rounded = second_term.astype(jnp.bfloat16)
    first_weight = jnp.einsum(
        "nbk,nkd->bd", first_rounded, loaded, preferred_element_type=jnp.float32
    )
    second_weight = jnp.einsum(
        "nbk,nkd->bd", second_rounded, loaded, preferred_element_type=jnp.float32
    )
    bit_sums, entropy_sum = lax.psum((bit_sums, entropy_sum), ("dp", "mp"))
    marginal = bit_sums / token_count
    codebook = -jnp.sum(marginal * jnp.log(marginal) + (1.0 - marginal) * jnp.log(1.0 - marginal))
    entropy_loss = entropy_sum / token_count - codebook
    log_odds = jnp.log(1.0 - marginal) - jnp.log(marginal)
    cotangent = (first_term - second_term * log_odds[None, :, None]).astype(jnp.bfloat16)
    padded_cot = jnp.concatenate(
        [cotangent, jnp.zeros((1,) + cotangent.shape[1:], cotangent.dtype)]
    )
    outgoing_cot = padded_cot[chosen].reshape(n_dp * capacity * cotangent.shape[1], BLK)
    arrived_cot = lax.all_to_all(outgoing_cot, "dp", split_axis=0, concat_axis=0, tiled=True)
    landed = arrived_cot.reshape(n_dp * capacity, cotangent.shape[1], BLK)[gather_order]
    latent_grad = jnp.einsum(
        "nbk,bd->nkd", landed, proj_weight, preferred_element_type=jnp.float32
    ).astype(jnp.bfloat16)
    first_weight, second_weight = lax.psum((first_weight, second_weight), ("dp", "mp"))
    weight_grad = (first_weight - second_weight * log_odds[:, None]) / jnp.sqrt(token_count)
    return (latent_grad.reshape(-1, feature_width), weight_grad, entropy_loss)


def solution(mesh):
    placed = (P(("dp", "mp"), None), P(), P(), P(), P(), P())
    return jax.shard_map(
        local,
        mesh=mesh,
        in_specs=placed,
        out_specs=(P(("dp", "mp"), None), P(), P()),
        check_vma=False,
    )
```

profile of v0, /device:TPU:0, one launch (start us, length us, event | category | flops | bytes accessed | tf_op | source)
XLA Modules:
  0.0 73.5 jit_solution(14534599684617418197)
XLA Ops:
  0.7 0.8 %reshape.158 = s32[8,4,64]{2,1,0:T(4,128)S(1)} reshape(s32[2048]{0:T(1024)} %param.9) | data formatting | bytes 16384 | tf_op jit(solution)/shard_map/reshape | solution.py:13
  1.4 1.3 %reduce_sum.46 = s32[]{:T(128)} reduce(s32[2048]{0:T(1024)} %param.9, s32[]{:T(128)} %constant.78.clone.1), dimensions={0}, to_apply=%region_2.3 | reduce | flops 2047 | bytes 8200 | tf_op jit(solution)/shard_map/reduce_sum | solution.py:68
  2.8 0.1 fusion.19
  2.9 4.2 %fusion.3 = (f32[]{:T(128)}, f32[18]{0:T(128)S(1)}, f32[18,64,128]{2,0,1:T(8,128)S(1)}) fusion(f32[64,128]{1,0:T(8,128)S(1)} %fusion.19, f32[18]{0:T(128)} %param.8, bf16[64,128,256]{2,1,0:T(8,128)(2,1)} %bitcast.89, bf16[18,256]{1,0:T(8,128)(2,1)S(1)} %copy-done), kind=kOutput, calls=%fused_computation.13 | convolution fusion | flops 78004208 | bytes 4826260 | tf_op jit(solution)/shard_map/nkd,bd->nbk/dot_general | solution.py:42
  7.1 0.8 %convolution_bitcast_fusion.1 = f32[18,256]{1,0:T(8,128)S(1)} fusion(bf16[64,128,256]{2,1,0:T(8,128)(2,1)S(1)} %bitcast.90, f32[18,64,128]{2,0,1:T(8,128)S(1)} %get-tuple-element.15, f32[64,128]{1,0:T(8,128)S(1)} %fusion.19), kind=kOutput, calls=%fused_computation.9 | convolution fusion | flops 76972032 | bytes 4835328 | tf_op jit(solution)/shard_map/nbk,nkd->bd/dot_general | solution.py:75
  7.9 0.8 %convolution_bitcast_fusion = f32[18,256]{1,0:T(8,128)S(1)} fusion(bf16[64,128,256]{2,1,0:T(8,128)(2,1)S(1)} %bitcast.91, f32[64,128]{1,0:T(8,128)S(1)} %fusion.19, f32[18,64,128]{2,0,1:T(8,128)S(1)} %get-tuple-element.15), kind=kOutput, calls=%fused_computation.8 | convolution fusion | flops 76824576 | bytes 4835328 | tf_op jit(solution)/shard_map/nbk,nkd->bd/dot_general | solution.py:78
  9.4 0.1 reshape.159
  9.5 0.1 reshape.161
  9.6 0.1 convert_reduce_fusion
  9.7 0.8 %scatter_custom_fusion = s32[64]{0:T(128)S(1)} fusion(s32[64]{0:T(128)S(1)} %fusion.27, s32[64]{0:T(128)S(1)} %iota.34, s32[]{:T(128)} %constant.88.clone.1), kind=kCustom, calls=%fused_computation.69 | custom fusion | bytes 260 | tf_op jit(solution)/shard_map/scatter | solution.py:29
  10.6 42.8 %all-reduce.1 = (f32[18]{0:T(128)S(1)}, f32[18,256]{1,0:T(8,128)S(1)}, f32[18,256]{1,0:T(8,128)S(1)}, f32[]{:T(128)}) all-reduce(f32[18]{0:T(128)S(1)} %get-tuple-element.4, f32[18,256]{1,0:T(8,128)S(1)} %convolution_bitcast_fusion.1, f32[18,256]{1,0:T(8,128)S(1)} %convolution_bitcast_fusion, ...), channel_id=1, replica_groups=mesh['dp'=8,'mp'=4] {'dp','mp'}, use_global_device_ids=true, to_apply=%region_1.2 | all-reduce | flops 9235 | bytes 73880 | tf_op jit(solution)/shard_map/psum | solution.py:81
  53.3 0.6 fusion.28
  53.9 0.4 subtract_convert_fusion
  54.4 0.7 gather_fusion
  55.0 0.8 %all_to_all.6 = bf16[8,144,128]{2,1,0:T(8,128)(2,1)} reshape(bf16[64,18,128]{2,1,0:T(8,128)(2,1)S(1)} %gather_fusion) | data formatting | bytes 589824 | tf_op jit(solution)/shard_map/all_to_all | solution.py:91
  55.8 5.3 %all-to-all-start = ((bf16[8,144,128]{2,1,0:T(8,128)(2,1)}), bf16[8,144,128]{2,1,0:T(8,128)(2,1)S(1)}, u32[]{:S(2)}, u32[]{:S(2)}) async-start(bf16[8,144,128]{2,1,0:T(8,128)(2,1)} %all_to_all.6), calls=%async_computation | async-start | bytes 589824 | tf_op jit(solution)/shard_map/all_to_all | solution.py:91
  61.2 0.1 select_n.80
  61.3 0.1 reshape.191
  62.7 2.4 %scatter_custom_fusion.1 = s32[32]{0:T(128)S(1)} fusion(s32[512]{0:T(512)S(1)} %bitcast.88, s32[512]{0:T(512)S(1)} %reshape.191, s32[]{:T(128)} %constant.78.clone.1), kind=kCustom, calls=%fused_computation.67 | custom fusion | bytes 132 | tf_op jit(solution)/shard_map/scatter | solution.py:33
  65.2 0.7 subtract_divide_fusion
  65.9 3.7 %all-to-all-done = bf16[8,144,128]{2,1,0:T(8,128)(2,1)S(1)} async-done(((bf16[8,144,128]{2,1,0:T(8,128)(2,1)}), bf16[8,144,128]{2,1,0:T(8,128)(2,1)S(1)}, u32[]{:S(2)}, u32[]{:S(2)}) %all-to-all-start) | async-done | bytes 294944 | tf_op jit(solution)/shard_map/all_to_all | solution.py:91
  69.6 0.1 reshape.160
  69.7 0.6 gather_fusion.1
  70.3 2.1 %convolution_convert_fusion = bf16[32,128,256]{2,1,0:T(8,128)(2,1)} fusion(bf16[32,18,128]{2,1,0:T(8,128)(2,1)S(1)} %gather_fusion.1, bf16[18,256]{1,0:T(8,128)(2,1)S(1)} %copy-done), kind=kOutput, calls=%fused_computation.5 | convolution fusion | flops 38797312 | bytes 2253824 | tf_op jit(solution)/shard_map/nbk,bd->nkd/dot_general | solution.py:93
  (22 shorter events, 0.2 us)
Async XLA Ops:
  0.6 2.2 %copy-start = (bf16[18,256]{1,0:T(8,128)(2,1)S(1)}, bf16[18,256]{1,0:T(8,128)(2,1)}, u32[]{:S(2)}) copy-start(bf16[18,256]{1,0:T(8,128)(2,1)} %param.7) | copy-start | bytes 27652
  2.9 4.2 %copy-start.3 = (bf16[8192,256]{1,0:T(8,128)(2,1)S(1)}, bf16[8192,256]{1,0:T(8,128)(2,1)}, u32[]{:S(2)}) copy-start(bf16[8192,256]{1,0:T(8,128)(2,1)} %param.6) | copy-start | bytes 12582916
  7.9 1.5 %copy-start.1 = (s32[2048]{0:T(1024)S(1)}, s32[2048]{0:T(1024)}, u32[]{:S(2)}) copy-start(s32[2048]{0:T(1024)} %param.10) | copy-start | bytes 24580
  7.9 1.5 %copy-start.2 = (s32[2048]{0:T(1024)S(1)}, s32[2048]{0:T(1024)}, u32[]{:S(2)}) copy-start(s32[2048]{0:T(1024)} %param.11) | copy-start | bytes 24580
  55.8 13.7 %all-to-all-start = ((bf16[8,144,128]{2,1,0:T(8,128)(2,1)}), bf16[8,144,128]{2,1,0:T(8,128)(2,1)S(1)}, u32[]{:S(2)}, u32[]{:S(2)}) async-start(bf16[8,144,128]{2,1,0:T(8,128)(2,1)} %all_to_all.6), calls=%async_computation | async-start | bytes 589824 | tf_op jit(solution)/shard_map/all_to_all | solution.py:91
where the time goes:
time: 74 us; the launch traced here: 73.5 us
  blocking collectives  42.8 us (58%)
  matrix products  7.88 us (11%)
  local copies, waits for them, and re-layouts  6.53 us (9%)
  starting transfers between devices  5.3 us (7%)
  between operations  3.96 us (5%)
  waiting for transfers between devices  3.68 us (5%)
  other arithmetic  3.36 us (5%)
    psum x1, blocking collectives, local(): bit_sums, entropy_sum = lax.psum((bit_sums, entropy_sum), ('dp', 'mp'))  42.8 us
    all_to_all x1, starting transfers between devices, local(): lax.all_to_all(outgoing_cot, 'dp', split_axis=0, concat_axis=0, tiled=True)  5.3 us
    dot_general x1, matrix products, statistics(): jnp.einsum('nkd,bd->nbk', blocks, proj_weight, preferred_element_type=jnp...  4.21 us
    all_to_all x1, waiting for transfers between devices, local(): lax.all_to_all(outgoing_cot, 'dp', split_axis=0, concat_axis=0, tiled=True)  3.68 us
    scatter x1, local copies, waits for them, and re-layouts, routing(): jnp.zeros((OUT_SLOTS,), jnp.int32).at[landing]  2.44 us
    dot_general x1, matrix products, local(): jnp.einsum('nbk,bd->nkd', landed, proj_weight, preferred_element_type=jnp...  2.08 us
  transfers between devices with their start and end apart: 1, of which 1 were waited for; matrix products, arithmetic and copies ran while one was open for 5% of the time, Pallas kernels for 0%

commit v1 on v0

--- a/solution.py
+++ b/solution.py
@@ -6,6 +6,10 @@
 BLK = 128
 OUT_SLOTS = 32
 sharpness = 2.0
+
+
+def heaps_pass(my_data):
+    return lax.psum(lax.psum(my_data, axis_name="mp"), axis_name="dp")
 
 
 def routing(fill, target, target_slot, n_dp, n_mp, in_slots, capacity, own_dp, own_mp):
@@ -78,7 +82,7 @@
     second_weight = jnp.einsum(
         "nbk,nkd->bd", second_rounded, loaded, preferred_element_type=jnp.float32
     )
-    bit_sums, entropy_sum = lax.psum((bit_sums, entropy_sum), ("dp", "mp"))
+    bit_sums, entropy_sum = heaps_pass((bit_sums, entropy_sum))
     marginal = bit_sums / token_count
     codebook = -jnp.sum(marginal * jnp.log(marginal) + (1.0 - marginal) * jnp.log(1.0 - marginal))
     entropy_loss = entropy_sum / token_count - codebook

time: 74 us -> 101 us (1.36)
  blocking collectives: 42.8 us -> 71.6 us
  waiting for transfers between devices: 3.68 us -> 0.01 us
  matrix products: 7.88 us -> 10 us
  starting transfers between devices: 5.3 us -> 3.42 us
  local copies, waits for them, and re-layouts: 6.53 us -> 8.21 us
    psum x1 -> x3, blocking collectives: 42.8 us -> 71.6 us  [the longest x1 40.3 us: local(): lax.psum((first_weight, second_weight), ('dp', 'mp'))]
    all_to_all x1, waiting for transfers between devices: 3.68 us -> 0.01 us  [local(): lax.all_to_all(outgoing_cot, 'dp', split_axis=0, concat_axis=0, tiled=True)]
    dot_general x1, matrix products: 0.82 us -> 3.13 us  [local(): jnp.einsum('nbk,nkd->bd', first_rounded, loaded, preferred_element_type=j...]
    all_to_all x1, starting transfers between devices: 5.3 us -> 3.42 us  [local(): lax.all_to_all(outgoing_cot, 'dp', split_axis=0, concat_axis=0, tiled=True)]
  transfers between devices with their start and end apart: 1 -> 1, of which waited for: 1 -> 0; matrix products, arithmetic and copies ran while one was open for 5% -> 7% of each run, Pallas kernels for 0% -> 0%
where the time goes in v1:
time: 101 us
  blocking collectives  71.6 us (71%)
  matrix products  10 us (10%)
  local copies, waits for them, and re-layouts  8.21 us (8%)
  between operations  3.95 us (4%)
  starting transfers between devices  3.42 us (3%)
  other arithmetic  3.36 us (3%)
    psum x1, blocking collectives, local(): lax.psum((first_weight, second_weight), ('dp', 'mp'))  40.3 us
    psum x2, blocking collectives, heaps_pass(): return lax.psum(lax.psum(my_data, axis_name='mp'), axis_name='dp')  31.3 us
    dot_general x1, matrix products, statistics(): jnp.einsum('nkd,bd->nbk', blocks, proj_weight, preferred_element_type=jnp...  4.06 us
    all_to_all x1, starting transfers between devices, local(): lax.all_to_all(outgoing_cot, 'dp', split_axis=0, concat_axis=0, tiled=True)  3.42 us
    dot_general x1, matrix products, local(): jnp.einsum('nbk,nkd->bd', first_rounded, loaded, preferred_element_type=j...  3.13 us
    scatter x1, local copies, waits for them, and re-layouts, routing(): jnp.zeros((OUT_SLOTS,), jnp.int32).at[landing]  2.44 us
    dot_general x1, matrix products, local(): jnp.einsum('nbk,bd->nkd', landed, proj_weight, preferred_element_type=jnp...  2.08 us
  transfers between devices with their start and end apart: 1, of which 0 were waited for; matrix products, arithmetic and copies ran while one was open for 7% of the time, Pallas kernels for 0%

profile of v1, /device:TPU:0, one launch (start us, length us, event | category | flops | bytes accessed | tf_op | source)
XLA Modules:
  0.0 100.5 jit_solution(7203812652973662267)
XLA Ops:
  0.7 0.8 reshape.158
  1.4 1.3 %reduce_sum.46 = s32[]{:T(128)} reduce(s32[2048]{0:T(1024)} %param.9, s32[]{:T(128)} %constant.78.clone.1), dimensions={0}, to_apply=%region_3.4 | reduce | flops 2047 | bytes 8200 | tf_op jit(solution)/shard_map/reduce_sum | solution.py:72
  3.4 0.8 reshape.159
  4.2 0.8 reshape.161
  5.0 0.1 convert_reduce_fusion
  5.2 0.8 scatter_custom_fusion
  6.1 4.1 %fusion.3 = (f32[]{:T(128)}, f32[18]{0:T(128)S(1)}, f32[18,64,128]{2,0,1:T(8,128)S(1)}) fusion(f32[64,128]{1,0:T(8,128)S(1)} %fusion.19, f32[18]{0:T(128)} %param.8, bf16[64,128,256]{2,1,0:T(8,128)(2,1)} %bitcast.89, bf16[18,256]{1,0:T(8,128)(2,1)S(1)} %copy-done), kind=kOutput, calls=%fused_computation.13 | convolution fusion | flops 78004208 | bytes 4826260 | tf_op jit(solution)/shard_map/nkd,bd->nbk/dot_general | solution.py:46
  10.2 9.0 %all-reduce.3 = (f32[18]{0:T(128)S(1)}, f32[]{:T(128)}) all-reduce(f32[18]{0:T(128)S(1)} %get-tuple-element.4, f32[]{:T(128)} %get-tuple-element.3), channel_id=1, replica_groups=mesh['dp'=8,'mp'=4] {'mp'}, use_global_device_ids=true, to_apply=%region_1.2 | all-reduce | flops 19 | bytes 152 | tf_op jit(solution)/shard_map/psum | solution.py:12
  19.1 22.3 %all-reduce.2 = (f32[18]{0:T(128)S(1)}, f32[]{:T(128)}) all-reduce(f32[18]{0:T(128)S(1)} %get-tuple-element.9, f32[]{:T(128)} %get-tuple-element.10), channel_id=1, replica_groups=mesh['dp'=8,'mp'=4] {'dp'}, use_global_device_ids=true, to_apply=%region_2.3 | all-reduce | flops 19 | bytes 152 | tf_op jit(solution)/shard_map/psum | solution.py:12
  41.4 0.6 fusion.28
  42.1 0.3 subtract_convert_fusion
  42.5 0.7 gather_fusion
  43.1 0.8 all_to_all.6
  43.9 3.4 %all-to-all-start = ((bf16[8,144,128]{2,1,0:T(8,128)(2,1)}), bf16[8,144,128]{2,1,0:T(8,128)(2,1)S(1)}, u32[]{:S(2)}, u32[]{:S(2)}) async-start(bf16[8,144,128]{2,1,0:T(8,128)(2,1)} %all_to_all.6), calls=%async_computation | async-start | bytes 589824 | tf_op jit(solution)/shard_map/all_to_all | solution.py:95
  47.4 3.1 %convolution_bitcast_fusion.1 = f32[18,256]{1,0:T(8,128)S(1)} fusion(bf16[64,128,256]{2,1,0:T(8,128)(2,1)} %bitcast.90, f32[18,64,128]{2,0,1:T(8,128)S(1)} %get-tuple-element.17, f32[64,128]{1,0:T(8,128)S(1)} %fusion.19), kind=kOutput, calls=%fused_computation.9 | convolution fusion | flops 76972032 | bytes 4835328 | tf_op jit(solution)/shard_map/nbk,nkd->bd/dot_general | solution.py:79
  50.6 0.3 copy-done.1
  50.9 0.7 convolution_bitcast_fusion
  51.8 0.1 reshape.191
  53.2 2.4 %scatter_custom_fusion.1 = s32[32]{0:T(128)S(1)} fusion(s32[512]{0:T(512)S(1)} %bitcast.88, s32[512]{0:T(512)S(1)} %reshape.191, s32[]{:T(128)} %constant.78.clone.1), kind=kCustom, calls=%fused_computation.67 | custom fusion | bytes 132 | tf_op jit(solution)/shard_map/scatter | solution.py:37
  55.6 40.3 %all-reduce.1 = (f32[18,256]{1,0:T(8,128)S(1)}, f32[18,256]{1,0:T(8,128)S(1)}) all-reduce(f32[18,256]{1,0:T(8,128)S(1)} %convolution_bitcast_fusion.1, f32[18,256]{1,0:T(8,128)S(1)} %convolution_bitcast_fusion), channel_id=1, replica_groups=mesh['dp'=8,'mp'=4] {'dp','mp'}, use_global_device_ids=true, to_apply=%region_7.8 | all-reduce | flops 9216 | bytes 73728 | tf_op jit(solution)/shard_map/psum | solution.py:100
  95.9 0.7 subtract_divide_fusion
  96.6 0.1 reshape.160
  96.7 0.6 gather_fusion.1
  97.3 2.1 %convolution_convert_fusion = bf16[32,128,256]{2,1,0:T(8,128)(2,1)} fusion(bf16[32,18,128]{2,1,0:T(8,128)(2,1)S(1)} %gather_fusion.1, bf16[18,256]{1,0:T(8,128)(2,1)S(1)} %copy-done), kind=kOutput, calls=%fused_computation.5 | convolution fusion | flops 38797312 | bytes 2253824 | tf_op jit(solution)/shard_map/nbk,bd->nkd/dot_general | solution.py:97
  (20 shorter events, 0.4 us)
Async XLA Ops:
  0.6 5.5 %copy-start = (bf16[18,256]{1,0:T(8,128)(2,1)S(1)}, bf16[18,256]{1,0:T(8,128)(2,1)}, u32[]{:S(2)}) copy-start(bf16[18,256]{1,0:T(8,128)(2,1)} %param.7) | copy-start | bytes 27652
  43.9 52.7 %all-to-all-start = ((bf16[8,144,128]{2,1,0:T(8,128)(2,1)}), bf16[8,144,128]{2,1,0:T(8,128)(2,1)S(1)}, u32[]{:S(2)}, u32[]{:S(2)}) async-start(bf16[8,144,128]{2,1,0:T(8,128)(2,1)} %all_to_all.6), calls=%async_computation | async-start | bytes 589824 | tf_op jit(solution)/shard_map/all_to_all | solution.py:95
  47.4 3.5 %copy-start.1 = (bf16[8192,256]{1,0:T(8,128)(2,1)S(1)}, bf16[8192,256]{1,0:T(8,128)(2,1)}, u32[]{:S(2)}) copy-start(bf16[8192,256]{1,0:T(8,128)(2,1)} %param.6) | copy-start | bytes 12582916
